TPU v7x, 256 devices: a whole 4x4x8 slice. The times are simulated.
256 devices in a mesh: blk: 32 (over z, x_lo, core), head: 8 (over x_hi, y).
Axes of the slice: x: 4 (x_hi: 2, x_lo: 2; x = x_hi * 2 + x_lo), y: 4, z: 8, core: 2. Of those that a mesh axis runs over, the one named last changes fastest.
Arguments:
- query_tokens: bfloat16 [16384, 3072], P(('blk', 'head')), may hold values from -12 to 12
- key_tokens: bfloat16 [16384, 3072], P(('blk', 'head')), may hold values from -6 to 6
- value_tokens: bfloat16 [16384, 3072], P(('blk', 'head')), may hold values from -6 to 6
- out_weight: bfloat16 [3072, 3072], P('head'), may hold values from -1.75 to 1.75
- kv_blocks: int32 [128, 16], P('blk'), may hold values from -1 to 127, as said below
Outputs:
- projected: bfloat16 [16384, 3072], P(('blk', 'head'))
Inputs may be any that keep to these rules, and one draw needn't show every extreme that they name: `kv_blocks`: row i lists the key blocks of 128 tokens that query block i attends to; let G = floor(i / 4). Entry 0 is i. Entry 1 is one of the blocks 4 * M to 4 * M + 3 with M = (G + 16) mod 32. Entry j >= 2 is -1 (absent) or one of the blocks 4 * (G + o) to 4 * (G + o) + 3, with o = j // 2 for even j and o = -(j - 1) // 2 for odd j; it is present whenever j < 8 and those blocks exist. Entries of one row are distinct.
All inputs are finite; a program needn't handle non-finite values.
Results may differ from a plain program's by a relative error of at most 0.012.
Values may be sent and summed in bfloat16 or wider, within the bound.
A program may use at most 128 MiB of HBM per device.

v0:
```python
import math
import jax
import jax.numpy as jnp
from jax import lax
from jax.sharding import PartitionSpec as P

HD = 128
masked_low = -1e30


def sparse_attend(query_sets, key_sets, value_sets, present):
    blocks_dev = present.shape[0]
    slots = present.shape[1]
    block_rows = query_sets.shape[2]
    scaling = 1.0 / math.sqrt(HD)
    allowed = jnp.broadcast_to(present[:, :, None], (blocks_dev, slots, block_rows)).reshape(
        blocks_dev, slots * block_rows
    )
    scores = (
        jnp.einsum("hbqd,hbkd->hbqk", query_sets, key_sets, preferred_element_type=jnp.float32)
        * scaling
    )
    mask_full = allowed[None, :, None, :]
    peak_value = jnp.max(jnp.where(mask_full, scores, masked_low), axis=-1, keepdims=True)
    weights = jnp.where(mask_full, jnp.exp(scores - peak_value), 0.0)
    denom = jnp.sum(weights, axis=-1)
    outputs = jnp.einsum(
        "hbqk,hbkd->hbqd",
        weights.astype(jnp.bfloat16),
        value_sets,
        preferred_element_type=jnp.float32,
    )
    return outputs / denom[..., None]


def on_device(query_tokens, key_tokens, value_tokens, out_weight, kv_blocks):
    queries, key_rows, value_rows = (
        lax.all_to_all(query_tokens, "head", split_axis=1, concat_axis=0, tiled=True),
        lax.all_to_all(key_tokens, "head", split_axis=1, concat_axis=0, tiled=True),
        lax.all_to_all(value_tokens, "head", split_axis=1, concat_axis=0, tiled=True),
    )
    row_total = queries.shape[0]
    feature_width = queries.shape[1]
    heads_dev = feature_width // HD
    blocks_dev = kv_blocks.shape[0]
    block_rows = row_total // blocks_dev
    slots = kv_blocks.shape[1]
    query_heads = queries.reshape(row_total, heads_dev, HD).transpose(1, 0, 2)
    query_sets = query_heads.reshape(heads_dev, blocks_dev, block_rows, HD)
    key_heads = key_rows.reshape(row_total, heads_dev, HD).transpose(1, 0, 2)
    value_heads = value_rows.reshape(row_total, heads_dev, HD).transpose(1, 0, 2)
    present = kv_blocks >= 0
    safe_index = jnp.maximum(kv_blocks, 0)
    gathered_keys, gathered_values = (
        lax.all_gather(key_heads, "blk", axis=1, tiled=True),
        lax.all_gather(value_heads, "blk", axis=1, tiled=True),
    )
    total_blocks = gathered_keys.shape[1] // block_rows
    source_keys = gathered_keys.reshape(heads_dev, total_blocks, block_rows, HD)
    source_values = gathered_values.reshape(heads_dev, total_blocks, block_rows, HD)
    flat_index = safe_index.reshape(blocks_dev * slots)
    key_sets = jnp.take(source_keys, flat_index, axis=1).reshape(
        heads_dev, blocks_dev, slots * block_rows, HD
    )
    value_sets = jnp.take(source_values, flat_index, axis=1).reshape(
        heads_dev, blocks_dev, slots * block_rows, HD
    )
    outputs = sparse_attend(query_sets, key_sets, value_sets, present)
    attended = (
        outputs.reshape(heads_dev, row_total, HD)
        .transpose(1, 0, 2)
        .reshape(row_total, feature_width)
    )
    attended = attended.astype(jnp.bfloat16)
    return lax.psum_scatter(
        jnp.dot(attended, out_weight, preferred_element_type=jnp.float32).astype(jnp.bfloat16),
        "head",
        scatter_dimension=0,
        tiled=True,
    )


def solution(mesh):
    placed = (
        P(("blk", "head"), None),
        P(("blk", "head"), None),
        P(("blk", "head"), None),
        P("head", None),
        P("blk", None),
    )
    return jax.shard_map(
        on_device, mesh=mesh, in_specs=placed, out_specs=P(("blk", "head"), None), check_vma=False
    )
```

profile of v0, /device:TPU:32, one launch (start us, length us, event | category | flops | bytes accessed | tf_op | source)
XLA Modules:
  0.0 322.1 jit_solution(16858350131159604797)
XLA Ops:
  6.5 0.0 copy-start
  6.5 0.0 copy-start.1
  6.5 0.0 all-gather.3.cloned.1.call-start
  6.5 1.2 copy.46
  7.7 16.9 %all_to_all.48 = bf16[64,8,384]{2,0,1:T(8,128)(2,1)S(1)} all-to-all(bf16[64,8,384]{2,0,1:T(8,128)(2,1)S(1)} %bitcast.64), channel_id=1, replica_groups=mesh['blk'=32,'head'=8] {'head'}, dimensions={1} | all-to-all | bytes 786432 | tf_op jit(solution)/shard_map/all_to_all | solution.py:39
  24.7 0.1 reshape.52
  24.8 0.8 copy.26
  25.6 0.0 all-gather.3.cloned.1.call-update
  25.6 0.0 all-gather.5.cloned.1.call-start
  25.6 1.0 copy.44
  26.7 12.0 %all_to_all.49 = bf16[64,8,384]{2,0,1:T(8,128)(2,1)S(1)} all-to-all(bf16[64,8,384]{2,0,1:T(8,128)(2,1)S(1)} %bitcast.65), channel_id=1, replica_groups=mesh['blk'=32,'head'=8] {'head'}, dimensions={1} | all-to-all | bytes 786432 | tf_op jit(solution)/shard_map/all_to_all | solution.py:40
  38.7 0.1 reshape.58
  38.8 0.8 copy.31
  39.7 0.0 all-gather.5.cloned.1.call-update
  39.7 1.9 copy.45
  41.5 3.5 %all-to-all-start.1 = ((bf16[64,8,384]{2,0,1:T(8,128)(2,1)}), bf16[64,8,384]{2,0,1:T(8,128)(2,1)S(1)}, u32[]{:S(2)}, u32[]{:S(2)}) async-start(bf16[64,8,384]{2,0,1:T(8,128)(2,1)} %bitcast.51), calls=%async_computation.1 | async-start | bytes 786432 | tf_op jit(solution)/shard_map/all_to_all | solution.py:38
  45.0 0.0 reduce-scatter.2.cloned.1.call-start
  45.1 0.0 copy-done.1
  45.1 0.1 reshape.54
  45.2 0.1 broadcast_bitcast_fusion
  45.3 8.9 %all-to-all-done.1 = bf16[64,8,384]{2,0,1:T(8,128)(2,1)S(1)} async-done(((bf16[64,8,384]{2,0,1:T(8,128)(2,1)}), bf16[64,8,384]{2,0,1:T(8,128)(2,1)S(1)}, u32[]{:S(2)}, u32[]{:S(2)}) %all-to-all-start.1) | async-done | bytes 393248 | tf_op jit(solution)/shard_map/all_to_all | solution.py:38
  54.2 0.1 reshape.56
  54.3 0.1 copy.29
  54.4 51.7 %all-gather.3.cloned.1.call-done = bf16[3,16384,128]{2,1,0:T(8,128)(2,1)} async-done(((bf16[3,512,128]{2,1,0:T(8,128)(2,1)}), bf16[3,16384,128]{2,1,0:T(8,128)(2,1)}) %all-gather.3.cloned.1.call-update) | async-done | bytes 12582928 | tf_op jit(solution)/shard_map/all_gather | solution.py:55
  106.1 8.6 %gather_fusion = bf16[64,3,128,128]{3,2,1,0:T(8,128)(2,1)} fusion(bf16[3,128,128,128]{3,2,1,0:T(8,128)(2,1)} %bitcast.56, s32[1024]{0:T(1024)S(1)} %pad_clamp_fusion), kind=kCustom, calls=%fused_computation.clone | custom fusion | bytes 12583168 | tf_op jit(solution)/shard_map/jit(_take)/gather | solution.py:62
  114.7 72.9 %all-gather.5.cloned.1.call-done = bf16[3,16384,128]{2,1,0:T(8,128)(2,1)} async-done(((bf16[3,512,128]{2,1,0:T(8,128)(2,1)}), bf16[3,16384,128]{2,1,0:T(8,128)(2,1)}) %all-gather.5.cloned.1.call-update) | async-done | bytes 12582928 | tf_op jit(solution)/shard_map/all_gather | solution.py:56
  187.6 8.5 %gather_fusion.1 = bf16[64,3,128,128]{3,2,1,0:T(8,128)(2,1)} fusion(bf16[3,128,128,128]{3,2,1,0:T(8,128)(2,1)} %bitcast.57, s32[1024]{0:T(1024)S(1)} %pad_clamp_fusion), kind=kCustom, calls=%fused_computation.1.clone | custom fusion | bytes 12583168 | tf_op jit(solution)/shard_map/jit(_take)/gather | solution.py:65
  196.1 5.5 %select_bitcast_fusion.1 = (bf16[3,64,128,128]{3,2,0,1:T(8,128)(2,1)S(1)}, bf16[3,64,128,128]{3,2,0,1:T(8,128)(2,1)S(1)}) fusion(bf16[64,3,128,128]{3,2,1,0:T(8,128)(2,1)} %gather_fusion, pred[64]{0:T(512)(128)(4,1)S(1)} %compare_and_fusion, bf16[64,3,128,128]{3,2,1,0:T(8,128)(2,1)} %gather_fusion.1), kind=kLoop, calls=%fused_computation.11 | loop fusion | flops 6291456 | bytes 25165888 | tf_op jit(solution)/shard_map/jit(_take)/select_n | solution.py:62
  201.7 4.0 %copy.27 = bf16[3,64,128,128]{3,2,1,0:T(8,128)(2,1)} copy(bf16[3,64,128,128]{3,2,0,1:T(8,128)(2,1)S(1)} %get-tuple-element.6) | data formatting | bytes 12582912 | tf_op jit(solution)/shard_map/jit(_take)/select_n | solution.py:62
  205.7 4.0 %copy.32 = bf16[3,64,128,128]{3,2,1,0:T(8,128)(2,1)} copy(bf16[3,64,128,128]{3,2,0,1:T(8,128)(2,1)S(1)} %get-tuple-element.7) | data formatting | bytes 12582912 | tf_op jit(solution)/shard_map/jit(_take)/select_n | solution.py:65
  209.7 10.3 %bitcast_reduce_fusion = (f32[3,4,128]{2,1,0:T(4,128)S(1)}, bf16[3,4,2048,128]{3,2,1,0:T(8,128)(2,1)}) fusion(pred[4,2048]{1,0:T(4,128)(4,1)S(1)} %bitcast.72, bf16[3,4,2048,128]{3,2,1,0:T(8,128)(2,1)} %bitcast.54, bf16[3,4,128,128]{3,2,1,0:T(8,128)(2,1)S(1)} %bitcast.66), kind=kOutput, calls=%fused_computation.3 | convolution fusion | flops 1632634880 | bytes 12990464 | tf_op jit(solution)/shard_map/sub | solution.py:25
  220.0 6.6 %fusion.10 = bf16[3,4,128,128]{3,2,1,0:T(8,128)(2,1)S(1)} fusion(bf16[3,4,2048,128]{3,2,1,0:T(8,128)(2,1)} %bitcast.55, f32[3,4,128]{2,1,0:T(4,128)S(1)} %get-tuple-element.8, bf16[3,4,2048,128]{3,2,1,0:T(8,128)(2,1)} %get-tuple-element.9), kind=kOutput, calls=%fused_computation.17 | convolution fusion | flops 805699584 | bytes 12982272 | tf_op jit(solution)/shard_map/hbqk,hbkd->hbqd/dot_general | solution.py:27
  226.7 0.2 copy.34
  226.9 0.0 copy-done
  226.9 3.5 %convolution_convert_fusion = bf16[512,3072]{1,0:T(8,128)(2,1)} fusion(bf16[512,384]{0,1:T(8,128)(2,1)S(1)} %bitcast.71, bf16[384,3072]{1,0:T(8,128)(2,1)S(1)} %copy-done), kind=kOutput, calls=%fused_computation.15 | convolution fusion | flops 1209532416 | bytes 5898240 | tf_op jit(solution)/shard_map/dot_general | solution.py:76
  230.3 0.0 reduce-scatter.2.cloned.1.call-update
  230.4 85.2 %reduce-scatter.2.cloned.1.call-done = bf16[64,3072]{1,0:T(8,128)(2,1)} async-done(((bf16[512,3072]{1,0:T(8,128)(2,1)}), bf16[64,3072]{1,0:T(8,128)(2,1)}) %reduce-scatter.2.cloned.1.call-update) | async-done | bytes 393232 | tf_op jit(solution)/shard_map/reduce_scatter | solution.py:75
  (6 shorter events, 0.0 us)
Async XLA Ops:
  6.5 220.3 %copy-start = (bf16[384,3072]{1,0:T(8,128)(2,1)S(1)}, bf16[384,3072]{1,0:T(8,128)(2,1)}, u32[]{:S(2)}) copy-start(bf16[384,3072]{1,0:T(8,128)(2,1)} %param.10) | copy-start | bytes 7077892
  6.5 38.5 %copy-start.1 = (s32[4,16]{1,0:T(4,128)S(1)}, s32[4,16]{1,0:T(4,128)}, u32[]{:S(2)}) copy-start(s32[4,16]{1,0:T(4,128)} %param.11) | copy-start | bytes 772
  6.5 99.5 %all-gather.3.cloned.1.call-start = ((), (), s32[]{:S(2)}) async-start(), calls=%async_computation.4 | async-start | bytes 12976128 | tf_op jit(solution)/shard_map/all_gather | solution.py:55
  25.6 162.0 %all-gather.5.cloned.1.call-start = ((), (), s32[]{:S(2)}) async-start(), calls=%async_computation.5 | async-start | bytes 12976128 | tf_op jit(solution)/shard_map/all_gather | solution.py:56
  41.5 12.6 %all-to-all-start.1 = ((bf16[64,8,384]{2,0,1:T(8,128)(2,1)}), bf16[64,8,384]{2,0,1:T(8,128)(2,1)S(1)}, u32[]{:S(2)}, u32[]{:S(2)}) async-start(bf16[64,8,384]{2,0,1:T(8,128)(2,1)} %bitcast.51), calls=%async_computation.1 | async-start | bytes 786432 | tf_op jit(solution)/shard_map/all_to_all | solution.py:38
  45.0 270.6 %reduce-scatter.2.cloned.1.call-start = ((), (), s32[]{:S(2)}) async-start(), calls=%async_computation.6 | async-start | bytes 3538944 | tf_op jit(solution)/shard_map/reduce_scatter | solution.py:75
Sparse Core Ops, SparseCore 0:
  25.7 80.2 all-gather.2
  107.9 79.6 all-gather.4
  230.5 85.0 reduce-scatter.1
where the time goes:
time: 323 us; the launch traced here: 322 us
  waiting for transfers between devices  219 us (68%)
  local copies, waits for them, and re-layouts  31.7 us (10%)
  blocking collectives  28.9 us (9%)
  matrix products  20.4 us (6%)
  between operations  13.2 us (4%)
  other arithmetic  5.58 us (2%)
  starting transfers between devices  3.54 us (1%)
    reduce_scatter x1, waiting for transfers between devices, on_device(): lax.psum_scatter(jnp.dot(attended, out_weight, preferred_element_type=jnp...  85.2 us
    all_gather x1, waiting for transfers between devices, on_device(): lax.all_gather(value_heads, 'blk', axis=1, tiled=True)  72.9 us
    all_gather x1, waiting for transfers between devices, on_device(): lax.all_gather(key_heads, 'blk', axis=1, tiled=True)  51.7 us
    all_to_all x1, blocking collectives, on_device(): lax.all_to_all(key_tokens, 'head', split_axis=1, concat_axis=0, tiled=True)  16.9 us
    all_to_all x1, blocking collectives, on_device(): lax.all_to_all(value_tokens, 'head', split_axis=1, concat_axis=0, tiled=T...  12 us
    sub x1, matrix products, sparse_attend(): weights = jnp.where(mask_full, jnp.exp(scores - peak_value), 0.0)  10.3 us
    all_to_all x1, waiting for transfers between devices, on_device(): lax.all_to_all(query_tokens, 'head', split_axis=1, concat_axis=0, tiled=T...  8.89 us
    gather x1, local copies, waits for them, and re-layouts, on_device(): jnp.take(source_keys, flat_index, axis=1)  8.63 us
  transfers between devices with their start and end apart: 4, of which 4 were waited for; matrix products, arithmetic and copies ran while one was open for 4% of the time, Pallas kernels for 0%

commit v1 on v0

--- a/solution.py
+++ b/solution.py
@@ -52,7 +52,9 @@
     present = kv_blocks >= 0
     safe_index = jnp.maximum(kv_blocks, 0)
     gathered_keys, gathered_values = (
-        lax.all_gather(key_heads, "blk", axis=1, tiled=True),
+        jnp.concatenate(
+            lax.all_to_all(jnp.stack([key_heads] * lax.axis_size("blk")), "blk", 0, 0), axis=1
+        ),
         lax.all_gather(value_heads, "blk", axis=1, tiled=True),
     )
     total_blocks = gathered_keys.shape[1] // block_rows

time: 323 us -> 558 us (1.73)
  waiting for transfers between devices: 219 us -> 442 us
  blocking collectives: 28.9 us -> 0 us
  starting transfers between devices: 3.54 us -> 23.7 us
  local copies, waits for them, and re-layouts: 31.7 us -> 51.8 us
    all_to_all x0 -> x3, waiting for transfers between devices: none -> 345 us  [the longest x1 329 us: on_device(): lax.all_to_all(jnp.stack([key_heads] * lax.axis_size('blk')), 'blk', 0, 0)]
    all_gather x1, waiting for transfers between devices: 72.9 us -> 0.01 us  [on_device(): lax.all_gather(value_heads, 'blk', axis=1, tiled=True)]
    all_gather x1 -> x0, waiting for transfers between devices: 51.7 us -> none  [on_device(): lax.all_gather(key_heads, 'blk', axis=1, tiled=True)]
    all_to_all x2 -> x0, blocking collectives: 28.9 us -> none  [the longest x1 16.9 us: on_device(): lax.all_to_all(key_tokens, 'head', split_axis=1, concat_axis=0, tiled=True)]
    all_to_all x0 -> x3, starting transfers between devices: none -> 19.3 us  [the longest x1 8.94 us: on_device(): lax.all_to_all(jnp.stack([key_heads] * lax.axis_size('blk')), 'blk', 0, 0)]
    all_to_all x0 -> x1, local copies, waits for them, and re-layouts: none -> 10.7 us  [on_device(): lax.all_to_all(jnp.stack([key_heads] * lax.axis_size('blk')), 'blk', 0, 0)]
    another operation x0 -> x1, local copies, waits for them, and re-layouts: none -> 7.7 us  [on_device(): jnp.stack([key_heads] * lax.axis_size('blk'))]
  transfers between devices with their start and end apart: 4 -> 6, of which waited for: 4 -> 5; matrix products, arithmetic and copies ran while one was open for 4% -> 5% of each run, Pallas kernels for 0% -> 0%
where the time goes in v1:
time: 558 us; the launch traced here: 557 us
  waiting for transfers between devices  442 us (79%)
  local copies, waits for them, and re-layouts  51.8 us (9%)
  starting transfers between devices  23.7 us (4%)
  matrix products  20.4 us (4%)
  between operations  13.6 us (2%)
  other arithmetic  5.58 us (1%)
    all_to_all x1, waiting for transfers between devices, on_device(): lax.all_to_all(jnp.stack([key_heads] * lax.axis_size('blk')), 'blk', 0, 0)  329 us
    reduce_scatter x1, waiting for transfers between devices, on_device(): lax.psum_scatter(jnp.dot(attended, out_weight, preferred_element_type=jnp...  88.8 us
  transfers between devices with their start and end apart: 6, of which 5 were waited for; matrix products, arithmetic and copies ran while one was open for 5% of the time, Pallas kernels for 0%

profile of v1, /device:TPU:32, one launch (start us, length us, event | category | flops | bytes accessed | tf_op | source)
XLA Modules:
  0.0 557.4 jit_solution(7965119695236095440)
XLA Ops:
  6.5 0.0 copy-start
  6.5 1.9 copy.48
  8.5 6.9 %all-to-all-start = ((bf16[64,8,384]{2,0,1:T(8,128)(2,1)}), bf16[64,8,384]{2,0,1:T(8,128)(2,1)S(1)}, u32[]{:S(2)}, u32[]{:S(2)}) async-start(bf16[64,8,384]{2,0,1:T(8,128)(2,1)} %bitcast.54), calls=%async_computation | async-start | bytes 786432 | tf_op jit(solution)/shard_map/all_to_all | solution.py:39
  15.4 1.8 copy.46
  17.2 8.2 %all-to-all-done = bf16[64,8,384]{2,0,1:T(8,128)(2,1)S(1)} async-done(((bf16[64,8,384]{2,0,1:T(8,128)(2,1)}), bf16[64,8,384]{2,0,1:T(8,128)(2,1)S(1)}, u32[]{:S(2)}, u32[]{:S(2)}) %all-to-all-start) | async-done | bytes 393248 | tf_op jit(solution)/shard_map/all_to_all | solution.py:39
  25.4 3.5 all-to-all-start.3
  28.8 1.8 copy.47
  30.6 7.6 %all-to-all-done.3 = bf16[64,8,384]{2,0,1:T(8,128)(2,1)S(1)} async-done(((bf16[64,8,384]{2,0,1:T(8,128)(2,1)}), bf16[64,8,384]{2,0,1:T(8,128)(2,1)S(1)}, u32[]{:S(2)}, u32[]{:S(2)}) %all-to-all-start.3) | async-done | bytes 393248 | tf_op jit(solution)/shard_map/all_to_all | solution.py:40
  38.2 0.0 copy-start.1
  38.2 4.1 all-to-all-start.2
  42.3 0.0 copy-done.1
  42.3 0.1 reshape.54
  42.4 0.1 copy.27
  42.5 9.1 %all-to-all-done.2 = bf16[64,8,384]{2,0,1:T(8,128)(2,1)} async-done(((bf16[64,8,384]{2,0,1:T(8,128)(2,1)}), bf16[64,8,384]{2,0,1:T(8,128)(2,1)}, u32[]{:S(2)}, u32[]{:S(2)}) %all-to-all-start.2) | async-done | bytes 393248 | tf_op jit(solution)/shard_map/all_to_all | solution.py:38
  51.6 7.7 %stack.2 = bf16[32,3,512,128]{3,2,1,0:T(8,128)(2,1)} broadcast(bf16[3,512,128]{2,1,0:T(8,128)(2,1)S(1)} %copy.27), dimensions={1,2,3} | broadcast | bytes 12976128 | tf_op jit(solution)/shard_map/stack | solution.py:56
  59.3 0.0 copy-start.2
  59.3 0.0 copy-start.3
  59.3 8.9 %all-to-all-start.1 = ((bf16[32,3,512,128]{3,2,1,0:T(8,128)(2,1)}), bf16[32,3,512,128]{3,2,1,0:T(8,128)(2,1)}, u32[]{:S(2)}, u32[]{:S(2)}) async-start(bf16[32,3,512,128]{3,2,1,0:T(8,128)(2,1)} %stack.2), calls=%async_computation.1 | async-start | bytes 25165824 | tf_op jit(solution)/shard_map/all_to_all | solution.py:56
  68.2 0.0 all-gather.2.cloned.1.call-start
  68.3 0.0 copy-done.2
  68.3 0.1 reshape.60
  68.4 0.8 copy.33
  69.2 0.0 all-gather.2.cloned.1.call-update
  69.2 0.2 reduce-scatter.2.cloned.1.call-start
  69.4 0.0 copy-done.3
  69.5 0.1 reshape.56
  69.6 0.1 broadcast_bitcast_fusion
  69.7 1.4 reshape.58
  71.1 0.1 copy.31
  71.2 328.8 %all-to-all-done.1 = bf16[32,3,512,128]{3,2,1,0:T(8,128)(2,1)} async-done(((bf16[32,3,512,128]{3,2,1,0:T(8,128)(2,1)}), bf16[32,3,512,128]{3,2,1,0:T(8,128)(2,1)}, u32[]{:S(2)}, u32[]{:S(2)}) %all-to-all-start.1) | async-done | bytes 12582944 | tf_op jit(solution)/shard_map/all_to_all | solution.py:56
  399.9 10.7 %copy.28 = bf16[32,3,512,128]{3,2,0,1:T(8,128)(2,1)} copy(bf16[32,3,512,128]{3,2,1,0:T(8,128)(2,1)} %all-to-all-done.1) | data formatting | bytes 25165824 | tf_op jit(solution)/shard_map/all_to_all | solution.py:56
  410.6 8.5 %gather_fusion = bf16[64,3,128,128]{3,2,1,0:T(8,128)(2,1)} fusion(bf16[3,128,128,128]{3,2,1,0:T(8,128)(2,1)} %bitcast.56, s32[1024]{0:T(1024)S(1)} %pad_clamp_fusion), kind=kCustom, calls=%fused_computation.clone | custom fusion | bytes 12583168 | tf_op jit(solution)/shard_map/jit(_take)/gather | solution.py:64
  419.1 0.0 all-gather.2.cloned.1.call-done
  419.1 8.5 %gather_fusion.1 = bf16[64,3,128,128]{3,2,1,0:T(8,128)(2,1)} fusion(bf16[3,128,128,128]{3,2,1,0:T(8,128)(2,1)} %bitcast.59, s32[1024]{0:T(1024)S(1)} %pad_clamp_fusion), kind=kCustom, calls=%fused_computation.1.clone | custom fusion | bytes 12583168 | tf_op jit(solution)/shard_map/jit(_take)/gather | solution.py:67
  427.6 5.5 select_bitcast_fusion.1
  433.2 4.0 copy.34
  437.2 4.0 copy.29
  441.2 10.3 %bitcast_reduce_fusion = (f32[3,4,128]{2,1,0:T(4,128)S(1)}, bf16[3,4,2048,128]{3,2,1,0:T(8,128)(2,1)}) fusion(pred[4,2048]{1,0:T(4,128)(4,1)S(1)} %bitcast.73, bf16[3,4,2048,128]{3,2,1,0:T(8,128)(2,1)} %bitcast.58, bf16[3,4,128,128]{3,2,1,0:T(8,128)(2,1)S(1)} %bitcast.67), kind=kOutput, calls=%fused_computation.3 | convolution fusion | flops 1632634880 | bytes 12990464 | tf_op jit(solution)/shard_map/sub | solution.py:25
  451.5 6.6 %fusion.10 = bf16[3,4,128,128]{3,2,1,0:T(8,128)(2,1)S(1)} fusion(bf16[3,4,2048,128]{3,2,1,0:T(8,128)(2,1)} %bitcast.57, f32[3,4,128]{2,1,0:T(4,128)S(1)} %get-tuple-element.8, bf16[3,4,2048,128]{3,2,1,0:T(8,128)(2,1)} %get-tuple-element.9), kind=kOutput, calls=%fused_computation.17 | convolution fusion | flops 805699584 | bytes 12982272 | tf_op jit(solution)/shard_map/hbqk,hbkd->hbqd/dot_general | solution.py:27
  458.1 0.2 copy.36
  458.3 0.0 copy-done
  458.3 3.5 convolution_convert_fusion
  461.8 0.0 reduce-scatter.2.cloned.1.call-update
  461.8 88.8 %reduce-scatter.2.cloned.1.call-done = bf16[64,3072]{1,0:T(8,128)(2,1)} async-done(((bf16[512,3072]{1,0:T(8,128)(2,1)}), bf16[64,3072]{1,0:T(8,128)(2,1)}) %reduce-scatter.2.cloned.1.call-update) | async-done | bytes 393232 | tf_op jit(solution)/shard_map/reduce_scatter | solution.py:77
  (6 shorter events, 0.0 us)
Async XLA Ops:
  6.5 451.8 %copy-start = (bf16[384,3072]{1,0:T(8,128)(2,1)S(1)}, bf16[384,3072]{1,0:T(8,128)(2,1)}, u32[]{:S(2)}) copy-start(bf16[384,3072]{1,0:T(8,128)(2,1)} %param.10) | copy-start | bytes 7077892
  8.5 16.9 %all-to-all-start = ((bf16[64,8,384]{2,0,1:T(8,128)(2,1)}), bf16[64,8,384]{2,0,1:T(8,128)(2,1)S(1)}, u32[]{:S(2)}, u32[]{:S(2)}) async-start(bf16[64,8,384]{2,0,1:T(8,128)(2,1)} %bitcast.54), calls=%async_computation | async-start | bytes 786432 | tf_op jit(solution)/shard_map/all_to_all | solution.py:39
  25.4 12.8 %all-to-all-start.3 = ((bf16[64,8,384]{2,0,1:T(8,128)(2,1)}), bf16[64,8,384]{2,0,1:T(8,128)(2,1)S(1)}, u32[]{:S(2)}, u32[]{:S(2)}) async-start(bf16[64,8,384]{2,0,1:T(8,128)(2,1)} %bitcast.66), calls=%async_computation.3 | async-start | bytes 786432 | tf_op jit(solution)/shard_map/all_to_all | solution.py:40
  38.2 4.1 copy-start.1
  38.2 13.4 %all-to-all-start.2 = ((bf16[64,8,384]{2,0,1:T(8,128)(2,1)}), bf16[64,8,384]{2,0,1:T(8,128)(2,1)}, u32[]{:S(2)}, u32[]{:S(2)}) async-start(bf16[64,8,384]{2,0,1:T(8,128)(2,1)} %bitcast.65), calls=%async_computation.2 | async-start | bytes 786432 | tf_op jit(solution)/shard_map/all_to_all | solution.py:38
  59.3 9.0 %copy-start.2 = (bf16[64,8,384]{2,0,1:T(8,128)(2,1)S(1)}, bf16[64,8,384]{2,0,1:T(8,128)(2,1)}, u32[]{:S(2)}) copy-start(bf16[64,8,384]{2,0,1:T(8,128)(2,1)} %copy-done.1) | copy-start | bytes 1179652
  59.3 10.2 %copy-start.3 = (s32[4,16]{1,0:T(4,128)S(1)}, s32[4,16]{1,0:T(4,128)}, u32[]{:S(2)}) copy-start(s32[4,16]{1,0:T(4,128)} %param.11) | copy-start | bytes 772
  59.3 340.7 %all-to-all-start.1 = ((bf16[32,3,512,128]{3,2,1,0:T(8,128)(2,1)}), bf16[32,3,512,128]{3,2,1,0:T(8,128)(2,1)}, u32[]{:S(2)}, u32[]{:S(2)}) async-start(bf16[32,3,512,128]{3,2,1,0:T(8,128)(2,1)} %stack.2), calls=%async_computation.1 | async-start | bytes 25165824 | tf_op jit(solution)/shard_map/all_to_all | solution.py:56
  68.2 350.9 %all-gather.2.cloned.1.call-start = ((), (), s32[]{:S(2)}) async-start(), calls=%async_computation.5 | async-start | bytes 12976128 | tf_op jit(solution)/shard_map/all_gather | solution.py:58
  69.2 481.4 %reduce-scatter.2.cloned.1.call-start = ((), (), s32[]{:S(2)}) async-start(), calls=%async_computation.6 | async-start | bytes 3538944 | tf_op jit(solution)/shard_map/reduce_scatter | solution.py:77
Sparse Core Ops, SparseCore 0:
  70.9 272.6 all-gather.1
  461.9 88.6 reduce-scatter.1
